TPU v7x, 256 devices: a whole 4x4x8 slice. The times are simulated.
256 devices in a mesh: ctx: 64 (over z, x, core), head: 4 (over y).
Axes of the slice: x: 4, y: 4, z: 8, core: 2. Of those that a mesh axis runs over, the one named last changes fastest.
Arguments:
- queries: float32 [16384, 4096], P('ctx', 'head'), may hold values from -48 to 48
- keys: float32 [16384, 4096], P('ctx', 'head'), may hold values from -48 to 48
- values: float32 [16384, 4096], P('ctx', 'head'), may hold values from -8 to 8
- query_map: float32 [32, 128, 128], P('head'), may hold values from -2 to 2
- key_map: float32 [32, 128, 128], P('head'), may hold values from -2 to 2
- out_weight: float32 [4096, 4096], P(None, ('ctx', 'head')), may hold values from -0.09375 to 0.09375
- residual: float32 [16384, 4096], P('ctx', 'head'), may hold values from -1.5 to 1.5
Outputs:
- layer_out: float32 [16384, 4096], P('ctx', 'head')
All inputs are finite; a program needn't handle non-finite values.
Results may differ from a plain program's by a relative error of at most 0.0001.
Values sent between devices are 32-bit elements; how exact they have to be, the bound alone decides.
A program may use at most 192 MiB of HBM per device.

v0:
```python
import jax
import jax.numpy as jnp
from jax import lax
from jax.sharding import PartitionSpec as P

HIGH = lax.Precision.HIGHEST


def carried_in(part, axis, combine, identity):
    place = lax.axis_index(axis)
    gathered = jax.tree.map(lambda a: lax.all_gather(a, axis), part)
    state = jax.tree.map(lambda a, e: jnp.zeros_like(a) + jnp.asarray(e, a.dtype), part, identity)

    def one(step, state):
        return combine(
            state, jax.tree.map(lambda a: lax.dynamic_index_in_dim(a, step, 0, False), gathered)
        )

    return lax.fori_loop(0, place, one, state)


def feature_map(inputs, weights):
    scores = jnp.einsum("nhd,hdf->hnf", inputs, weights, precision=HIGH)
    return jnp.concatenate(
        [jax.nn.softmax(scores, axis=-1), jax.nn.softmax(-scores, axis=-1)], axis=-1
    )


def add_pair(earlier, later):
    return (earlier[0] + later[0], earlier[1] + later[1])


def body(queries, keys, values, query_map, key_map, out_weight, residual):
    rows = queries.shape[0]
    heads_here, head_size, _ = query_map.shape
    width = heads_here * head_size
    shaped = (rows, heads_here, head_size)
    query_feat = feature_map(queries.reshape(shaped), query_map)
    key_feat = feature_map(keys.reshape(shaped), key_map)
    value_heads = values.reshape(shaped).transpose(1, 0, 2)
    local_state = jnp.einsum("hkf,hkd->hfd", key_feat, value_heads, precision=HIGH)
    local_norm = jnp.sum(key_feat, axis=1)
    zero_pair = (jnp.zeros_like(local_state), jnp.zeros_like(local_norm))
    prior_state, prior_norm = carried_in((local_state, local_norm), "ctx", add_pair, zero_pair)
    causal = jnp.tril(jnp.ones((rows, rows), jnp.float32))
    weights = jnp.einsum("hqf,hkf->hqk", query_feat, key_feat, precision=HIGH) * causal
    numer = jnp.einsum("hqk,hkd->hqd", weights, value_heads, precision=HIGH)
    numer = numer + jnp.einsum("hqf,hfd->hqd", query_feat, prior_state, precision=HIGH)
    denom = jnp.sum(weights, axis=-1) + jnp.einsum(
        "hqf,hf->hq", query_feat, prior_norm, precision=HIGH
    )
    mixed = (numer / denom[..., None]).transpose(1, 0, 2).reshape(rows, width)
    own_rows = lax.all_to_all(out_weight, "head", split_axis=0, concat_axis=1, tiled=True)
    partial_value = jnp.dot(
        mixed,
        lax.all_gather(own_rows, "ctx", axis=1, tiled=True),
        precision=HIGH,
        preferred_element_type=jnp.float32,
    )
    projected = lax.psum_scatter(partial_value, "head", scatter_dimension=1, tiled=True)
    return residual + projected


def solution(mesh):
    placed = (
        P("ctx", "head"),
        P("ctx", "head"),
        P("ctx", "head"),
        P("head", None, None),
        P("head", None, None),
        P(None, ("ctx", "head")),
        P("ctx", "head"),
    )
    return jax.shard_map(
        body, mesh=mesh, in_specs=placed, out_specs=P("ctx", "head"), check_vma=False
    )
```

profile of v0, /device:TPU:1, one launch (start us, length us, event | category | flops | bytes accessed | tf_op | source)
XLA Modules:
  0.0 486.4 jit_solution(5535288748645154746)
XLA Ops:
  6.5 1.2 copy-done
  7.8 2.1 fusion.29
  9.9 1.1 fusion.46
  11.0 1.1 fusion.47
  12.3 1.3 copy-done.6
  13.6 3.0 fusion.24
  16.7 10.4 %all_to_all.19 = f32[4,1024,16]{1,2,0:T(8,128)} all-to-all(f32[4,1024,16]{1,2,0:T(8,128)S(1)} %bitcast.68), channel_id=1, replica_groups=mesh['ctx'=64,'head'=4] {'head'}, dimensions={0} | all-to-all | bytes 524288 | tf_op jit(solution)/shard_map/all_to_all | solution.py:53
  27.2 2.5 copy.70
  30.1 60.9 %all-gather.1 = f32[512,256]{1,0:T(8,128)} all-gather(f32[8,256]{1,0:T(8,128)S(1)} %fusion.23), channel_id=3, replica_groups=mesh['ctx'=64,'head'=4] {'ctx'}, dimensions={0}, use_global_device_ids=true | all-gather | bytes 532480 | tf_op jit(solution)/shard_map/all_gather | solution.py:11
  91.1 1.1 fusion.32
  92.2 1.1 fusion.48
  93.3 1.1 fusion.49
  94.6 1.0 copy-done.1
  96.0 4.8 multiply_reduce_fusion
  100.8 157.3 %all-gather.7.cloned.1.call-done = f32[512,256,128]{2,1,0:T(8,128)} async-done(((f32[8,256,128]{2,1,0:T(8,128)}), f32[512,256,128]{2,1,0:T(8,128)}) %all-gather.7.cloned.1.call-update) | async-done | bytes 67108880 | tf_op jit(solution)/shard_map/all_gather | solution.py:11
  258.2 2.4 while.12
  258.4 1.5 bitcast_add_fusion.5
  260.6 2.5 fusion.26
  263.1 2.0 fusion.27
  265.2 2.2 fusion.20
  267.4 89.8 %all-gather.5.cloned.1.call-done = f32[1024,4096]{0,1:T(8,128)} async-done(((f32[1024,64]{0,1:T(8,128)}), f32[1024,4096]{0,1:T(8,128)}) %all-gather.5.cloned.1.call-update) | async-done | bytes 16777232 | tf_op jit(solution)/shard_map/all_gather | solution.py:56
  357.2 30.4 %fusion.50 = f32[256,4096]{1,0:T(8,128)} fusion(f32[256,1024]{0,1:T(8,128)S(1)} %bitcast.64, f32[1024,4096]{0,1:T(8,128)} %all-gather.5.cloned.1.call-done), kind=kOutput, calls=%fused_computation.59 | convolution fusion | flops 12884901888 | bytes 22020096 | tf_op jit(solution)/shard_map/dot_general | solution.py:54
  387.6 89.9 %reduce-scatter.2.cloned.1.call-done = f32[256,1024]{1,0:T(8,128)} async-done(((f32[256,4096]{1,0:T(8,128)}), f32[256,1024]{1,0:T(8,128)}) %reduce-scatter.2.cloned.1.call-update) | async-done | bytes 1048592 | tf_op jit(solution)/shard_map/reduce_scatter | solution.py:60
  477.6 2.3 add.38
  (36 shorter events, 2.0 us)
Async XLA Ops:
  6.5 1.2 copy-start
  6.5 251.6 %all-gather.7.cloned.1.call-start = ((), (), s32[]{:S(2)}) async-start(), calls=%async_computation.4 | async-start | bytes 68157440 | tf_op jit(solution)/shard_map/all_gather | solution.py:11
  12.1 1.5 copy-start.6
  12.3 17.4 %copy-start.3 = (f32[8,256,128]{1,2,0:T(8,128)}, f32[8,256,128]{1,2,0:T(8,128)S(1)}, u32[]{:S(2)}) copy-start(f32[8,256,128]{1,2,0:T(8,128)S(1)} %get-tuple-element.64) | copy-start | bytes 3145732
  13.6 3.0 copy-start.11
  16.6 340.6 %all-gather.5.cloned.1.call-start = ((), (), s32[]{:S(2)}) async-start(), calls=%async_computation.2 | async-start | bytes 17039360 | tf_op jit(solution)/shard_map/all_gather | solution.py:56
  27.1 450.4 %reduce-scatter.2.cloned.1.call-start = ((), (), s32[]{:S(2)}) async-start(), calls=%async_computation.3 | async-start | bytes 5242880 | tf_op jit(solution)/shard_map/reduce_scatter | solution.py:60
  27.2 63.9 %copy-start.9 = (f32[256,1024]{1,0:T(8,128)S(1)}, f32[256,1024]{1,0:T(8,128)}, u32[]{:S(2)}) copy-start(f32[256,1024]{1,0:T(8,128)} %param.9) | copy-start | bytes 3145732
  27.2 63.9 %copy-start.10 = (f32[8,128,128]{2,1,0:T(8,128)S(1)}, f32[8,128,128]{2,1,0:T(8,128)}, u32[]{:S(2)}) copy-start(f32[8,128,128]{2,1,0:T(8,128)} %param.12) | copy-start | bytes 1572868
  94.4 1.5 copy-start.4
  94.6 1.0 copy-start.1
  260.6 2.5 copy-start.2
  263.1 2.0 copy-start.5
  263.1 2.0 copy-start.7
  387.6 90.0 %copy-start.8 = (f32[256,1024]{1,0:T(8,128)S(1)}, f32[256,1024]{1,0:T(8,128)}, u32[]{:S(2)}) copy-start(f32[256,1024]{1,0:T(8,128)} %param.15) | copy-start | bytes 3145732
Sparse Core Ops, SparseCore 0:
  16.7 241.3 all-gather.6
  260.9 96.2 all-gather.4
  387.7 89.7 reduce-scatter.1
where the time goes:
time: 492 us; the launch traced here: 486 us
  waiting for transfers between devices  337 us (68%)
  blocking collectives  71.4 us (15%)
  matrix products  48.2 us (10%)
  between operations  13.3 us (3%)
  other arithmetic  9.65 us (2%)
  local copies, waits for them, and re-layouts  6.49 us (1%)
    all_gather x1, waiting for transfers between devices, carried_in(): gathered = jax.tree.map(lambda a: lax.all_gather(a, axis), part)  157 us
    reduce_scatter x1, waiting for transfers between devices, body(): lax.psum_scatter(partial_value, 'head', scatter_dimension=1, tiled=True)  89.9 us
    all_gather x1, waiting for transfers between devices, body(): lax.all_gather(own_rows, 'ctx', axis=1, tiled=True)  89.8 us
    all_gather x1, blocking collectives, carried_in(): gathered = jax.tree.map(lambda a: lax.all_gather(a, axis), part)  60.9 us
    dot_general x1, matrix products, body(): jnp.dot(mixed, lax.all_gather(own_rows, 'ctx', axis=1, tiled=True), preci...  30.4 us
    all_to_all x1, blocking collectives, body(): lax.all_to_all(out_weight, 'head', split_axis=0, concat_axis=1, tiled=True)  10.4 us
  transfers between devices with their start and end apart: 3, of which 3 were waited for; matrix products, arithmetic and copies ran while one was open for 4% of the time, Pallas kernels for 0%

commit v1 on v0

--- a/solution.py
+++ b/solution.py
@@ -53,7 +53,9 @@
     own_rows = lax.all_to_all(out_weight, "head", split_axis=0, concat_axis=1, tiled=True)
     partial_value = jnp.dot(
         mixed,
-        lax.all_gather(own_rows, "ctx", axis=1, tiled=True),
+        jnp.concatenate(
+            lax.all_to_all(jnp.stack([own_rows] * lax.axis_size("ctx")), "ctx", 0, 0), axis=1
+        ),
         precision=HIGH,
         preferred_element_type=jnp.float32,
     )

time: 492 us -> 869 us (1.77)
  blocking collectives: 71.4 us -> 583 us
  waiting for transfers between devices: 337 us -> 180 us
  starting transfers between devices: 0.09 us -> 13.7 us
  local copies, waits for them, and re-layouts: 6.49 us -> 15.2 us
    all_gather x1, blocking collectives: 60.9 us -> 572 us  [carried_in(): gathered = jax.tree.map(lambda a: lax.all_gather(a, axis), part)]
    all_gather x1, waiting for transfers between devices: 157 us -> 0.01 us  [carried_in(): gathered = jax.tree.map(lambda a: lax.all_gather(a, axis), part)]
    reduce_scatter x1, waiting for transfers between devices: 89.9 us -> 180 us  [body(): lax.psum_scatter(partial_value, 'head', scatter_dimension=1, tiled=True)]
    all_gather x1 -> x0, waiting for transfers between devices: 89.8 us -> none  [body(): lax.all_gather(own_rows, 'ctx', axis=1, tiled=True)]
    all_to_all x0 -> x1, starting transfers between devices: none -> 13.6 us  [body(): lax.all_to_all(jnp.stack([own_rows] * lax.axis_size('ctx')), 'ctx', 0, 0)]
    another operation x0 -> x1, local copies, waits for them, and re-layouts: none -> 8.76 us  [body(): jnp.stack([own_rows] * lax.axis_size('ctx'))]
  transfers between devices with their start and end apart: 3 -> 3, of which waited for: 3 -> 1; matrix products, arithmetic and copies ran while one was open for 4% -> 3% of each run, Pallas kernels for 0% -> 0%
where the time goes in v1:
time: 869 us; the launch traced here: 863 us
  blocking collectives  583 us (67%)
  waiting for transfers between devices  180 us (21%)
  matrix products  48.5 us (6%)
  local copies, waits for them, and re-layouts  15.2 us (2%)
  starting transfers between devices  13.7 us (2%)
  between operations  13.6 us (2%)
  other arithmetic  9.65 us (1%)
    all_gather x1, blocking collectives, carried_in(): gathered = jax.tree.map(lambda a: lax.all_gather(a, axis), part)  572 us
    reduce_scatter x1, waiting for transfers between devices, body(): lax.psum_scatter(partial_value, 'head', scatter_dimension=1, tiled=True)  180 us
    dot_general x1, matrix products, body(): jnp.dot(mixed, jnp.concatenate(lax.all_to_all(jnp.stack([own_rows] * lax....  30.7 us
  transfers between devices with their start and end apart: 3, of which 1 were waited for; matrix products, arithmetic and copies ran while one was open for 3% of the time, Pallas kernels for 0%

profile of v1, /device:TPU:1, one launch (start us, length us, event | category | flops | bytes accessed | tf_op | source)
XLA Modules:
  0.0 863.0 jit_solution(18222511581191667597)
XLA Ops:
  6.5 1.2 copy-done
  7.8 2.1 fusion.29
  9.9 1.1 fusion.46
  11.0 1.1 fusion.47
  12.3 1.3 copy-done.6
  13.6 3.0 fusion.24
  16.6 10.4 %all_to_all.21 = f32[4,1024,16]{1,2,0:T(8,128)S(1)} all-to-all(f32[4,1024,16]{1,2,0:T(8,128)S(1)} %bitcast.71), channel_id=1, replica_groups=mesh['ctx'=64,'head'=4] {'head'}, dimensions={0} | all-to-all | bytes 524288 | tf_op jit(solution)/shard_map/all_to_all | solution.py:53
  27.0 8.8 %stack.5 = f32[64,1024,64]{1,2,0:T(8,128)} broadcast(f32[1024,64]{0,1:T(8,128)S(1)} %bitcast.70), dimensions={1,2} | broadcast | bytes 17039360 | tf_op jit(solution)/shard_map/stack | solution.py:57
  35.7 13.6 %all-to-all-start.1 = ((f32[64,1024,64]{1,2,0:T(8,128)}), f32[64,1024,64]{1,2,0:T(8,128)}, u32[]{:S(2)}, u32[]{:S(2)}) async-start(f32[64,1024,64]{1,2,0:T(8,128)} %stack.5), calls=%async_computation.1 | async-start | bytes 33554432 | tf_op jit(solution)/shard_map/all_to_all | solution.py:57
  49.5 2.5 copy.70
  52.4 572.2 %all-gather.1 = f32[512,256]{1,0:T(8,128)} all-gather(f32[8,256]{1,0:T(8,128)S(1)} %fusion.23), channel_id=3, replica_groups=mesh['ctx'=64,'head'=4] {'ctx'}, dimensions={0}, use_global_device_ids=true | all-gather | bytes 532480 | tf_op jit(solution)/shard_map/all_gather | solution.py:11
  624.6 1.1 fusion.32
  625.8 1.1 fusion.48
  626.9 1.1 fusion.49
  628.2 1.0 copy-done.1
  629.5 4.8 multiply_reduce_fusion
  634.4 2.2 while.12
  634.4 1.5 bitcast_add_fusion.5
  636.6 2.5 fusion.26
  639.1 2.0 fusion.27
  641.2 2.2 fusion.20
  643.4 30.7 %fusion.50 = f32[256,4096]{1,0:T(8,128)} fusion(f32[256,1024]{0,1:T(8,128)S(1)} %bitcast.67, f32[1024,4096]{0,1:T(8,128)} %bitcast.14), kind=kOutput, calls=%fused_computation.59 | convolution fusion | flops 12884901888 | bytes 22020096 | tf_op jit(solution)/shard_map/dot_general | solution.py:54
  674.1 179.7 %reduce-scatter.2.cloned.1.call-done = f32[256,1024]{1,0:T(8,128)} async-done(((f32[256,4096]{1,0:T(8,128)}), f32[256,1024]{1,0:T(8,128)}) %reduce-scatter.2.cloned.1.call-update) | async-done | bytes 1048592 | tf_op jit(solution)/shard_map/reduce_scatter | solution.py:62
  853.9 2.3 add.38
  (36 shorter events, 2.0 us)
Async XLA Ops:
  6.5 1.2 copy-start
  6.5 627.8 %all-gather.4.cloned.1.call-start = ((), (), s32[]{:S(2)}) async-start(), calls=%async_computation.4 | async-start | bytes 68157440 | tf_op jit(solution)/shard_map/all_gather | solution.py:11
  12.1 1.5 copy-start.6
  12.3 39.7 %copy-start.3 = (f32[8,256,128]{1,2,0:T(8,128)}, f32[8,256,128]{1,2,0:T(8,128)S(1)}, u32[]{:S(2)}) copy-start(f32[8,256,128]{1,2,0:T(8,128)S(1)} %get-tuple-element.64) | copy-start | bytes 3145732
  13.6 3.0 copy-start.11
  35.7 607.6 %all-to-all-start.1 = ((f32[64,1024,64]{1,2,0:T(8,128)}), f32[64,1024,64]{1,2,0:T(8,128)}, u32[]{:S(2)}, u32[]{:S(2)}) async-start(f32[64,1024,64]{1,2,0:T(8,128)} %stack.5), calls=%async_computation.1 | async-start | bytes 33554432 | tf_op jit(solution)/shard_map/all_to_all | solution.py:57
  49.4 804.5 %reduce-scatter.2.cloned.1.call-start = ((), (), s32[]{:S(2)}) async-start(), calls=%async_computation.3 | async-start | bytes 5242880 | tf_op jit(solution)/shard_map/reduce_scatter | solution.py:62
  49.4 575.2 %copy-start.9 = (f32[256,1024]{1,0:T(8,128)S(1)}, f32[256,1024]{1,0:T(8,128)}, u32[]{:S(2)}) copy-start(f32[256,1024]{1,0:T(8,128)} %param.9) | copy-start | bytes 3145732
  49.4 575.2 %copy-start.10 = (f32[8,128,128]{2,1,0:T(8,128)S(1)}, f32[8,128,128]{2,1,0:T(8,128)}, u32[]{:S(2)}) copy-start(f32[8,128,128]{2,1,0:T(8,128)} %param.12) | copy-start | bytes 1572868
  628.0 1.5 copy-start.4
  628.2 1.0 copy-start.1
  636.6 2.5 copy-start.2
  639.1 2.0 copy-start.5
  639.1 2.0 copy-start.7
  674.1 179.8 %copy-start.8 = (f32[256,1024]{1,0:T(8,128)S(1)}, f32[256,1024]{1,0:T(8,128)}, u32[]{:S(2)}) copy-start(f32[256,1024]{1,0:T(8,128)} %param.15) | copy-start | bytes 3145732
Sparse Core Ops, SparseCore 0:
  16.7 583.3 all-gather.3
  674.3 179.5 reduce-scatter.1
